TPU v7x, 256 devices: a whole 4x4x8 slice. The times are simulated.
256 devices in a mesh: chan: 32 (over z, y_hi, core), tm: 8 (over y_lo, x).
Axes of the slice: x: 4, y: 4 (y_hi: 2, y_lo: 2; y = y_hi * 2 + y_lo), z: 8, core: 2. Of those that a mesh axis runs over, the one named last changes fastest.
Arguments:
- traces: bfloat16 [32, 192, 128, 1024], P('chan', 'tm'), may hold values from -6 to 6
- valid_mask: int32 [32, 192, 1024], P('chan', 'tm'), may hold values 0 or 1
- pair_owner: int32 [32, 4], P('chan'), may hold values from -1 to 31, as said below
Outputs:
- correlations: float32 [32, 4, 101, 128], P('chan')
Inputs may be any that keep to these rules, and one draw needn't show every extreme that they name: `pair_owner`: row r lists distinct owners in r + 1 .. r + 4 (within the cable) in its leading slots, then -1; every reader with a block above it has one pair or more, and reader 0 fills all 4 slots.
All inputs are finite; a program needn't handle non-finite values. No bound on the sum of `valid_mask` on one device may be relied on, other than what follows from the above.
Results may differ from a plain program's by a relative error of at most 0.0052.
Values may be sent and summed in bfloat16 or wider, within the bound.
No kernel may reach another device: no remote copies, remote signals or barrier semaphores. Data moves between devices by JAX's collectives and lax.ppermute only.
A program may use at most 64 MiB of HBM per device.

v0:
```python
import math
import jax
import jax.numpy as jnp
from jax import lax
from jax.sharding import PartitionSpec as P

NF = 256
MAXLAG = 50
SMOOTH = 4
REACH = 4
water_level = 0.05
eps = 1e-06


def shifted(block, axis, distance):
    devices = range(lax.axis_size(axis))
    route = [(i - distance, i) for i in devices if i - distance in devices]
    return lax.ppermute(block, axis, route)


def forward_table(samples_count, bins_count):
    samples = jnp.arange(samples_count, dtype=jnp.int32)
    bins = jnp.arange(1, bins_count + 1, dtype=jnp.int32)
    phase = samples[:, None] * bins[None, :] % samples_count
    angle = phase.astype(jnp.float32) * jnp.float32(2.0 * math.pi / samples_count)
    return jnp.concatenate([jnp.cos(angle), -jnp.sin(angle)], axis=1).astype(jnp.bfloat16)


def inverse_table(samples_count, bins_count, windows_all):
    bins = jnp.arange(1, bins_count + 1, dtype=jnp.int32)
    offsets = jnp.arange(2 * MAXLAG + 1, dtype=jnp.int32) - MAXLAG
    phase = bins[:, None] * offsets[None, :] % samples_count
    angle = phase.astype(jnp.float32) * jnp.float32(2.0 * math.pi / samples_count)
    factor = jnp.float32(1.0 / math.sqrt(windows_all * bins_count))
    return jnp.concatenate([jnp.cos(angle), -jnp.sin(angle)], axis=0) * factor


def whiten(block_traces, block_mask, forward, bins_count):
    masked = block_traces * block_mask[:, None, :].astype(jnp.bfloat16)
    wins, chans, samples = masked.shape
    spectra = jnp.dot(
        masked.reshape(wins * chans, samples), forward, preferred_element_type=jnp.float32
    )
    spectra = spectra.reshape(wins, chans, 2 * bins_count)
    real_part = spectra[..., :bins_count]
    imag_part = spectra[..., bins_count:]
    amplitude = jnp.sqrt(real_part * real_part + imag_part * imag_part)
    padded = jnp.pad(amplitude, ((0, 0), (0, 0), (SMOOTH, SMOOTH)))
    smooth = padded[..., 0:bins_count]
    for j in range(1, 2 * SMOOTH + 1):
        smooth = smooth + padded[..., j : j + bins_count]
    smooth = smooth / jnp.float32(2 * SMOOTH + 1)
    divisor = smooth + water_level * jnp.mean(amplitude, axis=-1, keepdims=True) + eps
    return (spectra / jnp.concatenate([divisor, divisor], axis=-1)).astype(jnp.bfloat16)


def cross_spectrum(own_spec, other_spec, bins_count):
    swapped = jnp.concatenate([other_spec[..., bins_count:], other_spec[..., :bins_count]], axis=-1)
    direct = jnp.einsum("wcf,wcf->cf", own_spec, other_spec, preferred_element_type=jnp.float32)
    crossed = jnp.einsum("wcf,wcf->cf", own_spec, swapped, preferred_element_type=jnp.float32)
    return jnp.concatenate(
        [
            direct[:, :bins_count] + direct[:, bins_count:],
            crossed[:, :bins_count] - crossed[:, bins_count:],
        ],
        axis=-1,
    )


def body(traces, valid_mask, pair_owner):
    wins_here = traces.shape[1]
    samples_count = traces.shape[3]
    bins_count = NF
    windows_all = wins_here * lax.axis_size("tm")
    forward = forward_table(samples_count, bins_count)
    inverse = inverse_table(samples_count, bins_count, windows_all)
    own_spec = whiten(traces[0], valid_mask[0], forward, bins_count)
    reader = lax.axis_index("chan")
    owners = pair_owner[0]
    chans = own_spec.shape[1]
    stacks = jnp.zeros((REACH, chans, 2 * bins_count), jnp.float32)
    for distance in range(1, REACH + 1):
        arrived = shifted(own_spec, "chan", -distance)
        chosen = (owners == reader + distance).astype(jnp.float32)
        cross = cross_spectrum(own_spec, arrived, bins_count)
        stacks = stacks + chosen[:, None, None] * cross[None, :, :]
    summed = lax.psum(stacks, "tm")
    result = jnp.einsum("pck,kl->plc", summed, inverse, precision=lax.Precision.HIGHEST)
    return result[None]


def solution(mesh):
    return jax.shard_map(
        body,
        mesh=mesh,
        in_specs=(P("chan", "tm", None, None), P("chan", "tm", None), P("chan", None)),
        out_specs=P("chan", None, None, None),
        check_vma=False,
    )
```

profile of v0, /device:TPU:32, one launch (start us, length us, event | category | flops | bytes accessed | tf_op | source)
XLA Modules:
  0.0 380.4 jit_solution(3332210686201202869)
XLA Ops:
  6.5 4.4 %cosine_convert_fusion = (bf16[1024,256]{1,0:T(8,128)(2,1)S(1)}, bf16[1024,256]{1,0:T(8,128)(2,1)S(1)}) fusion(s32[256]{0:T(256)S(1)} %iota_add_fusion), kind=kLoop, calls=%fused_computation.60 | loop fusion | flops 4456448 | bytes 1049600 | tf_op jit(solution)/shard_map/convert.4
  11.0 0.9 convert_bitcast_fusion
  11.9 5.6 %fusion.9 = f32[24,128,512]{2,1,0:T(8,128)S(1)} fusion(bf16[1,24,128,1024]{3,2,1,0:T(8,128)(2,1)} %param.3, bf16[24,1024]{1,0:T(8,128)(2,1)S(1)} %convert_bitcast_fusion, bf16[1024,256]{1,0:T(8,128)(2,1)S(1)} %get-tuple-element.26, bf16[1024,256]{1,0:T(8,128)(2,1)S(1)} %get-tuple-element.25), kind=kOutput, calls=%fused_computation.27 | convolution fusion | flops 3226468352 | bytes 13680640 | tf_op jit(solution)/shard_map/dot_general | solution.py:41
  17.4 1.2 fusion.48
  18.6 8.2 %fusion.20 = f32[24,128,256]{2,1,0:T(8,128)} fusion(f32[24,128,256]{2,1,0:T(8,128)S(1)} %get-tuple-element.14, f32[24,128]{1,0:T(8,128)S(1)} %broadcast_multiply_fusion), kind=kLoop, calls=%fused_computation.38 | loop fusion | flops 8650752 | bytes 6303744 | tf_op jit(solution)/shard_map/add | solution.py:53
  26.9 5.0 %fusion.8 = bf16[24,128,512]{2,1,0:T(8,128)(2,1)} fusion(f32[24,128,512]{2,1,0:T(8,128)S(1)} %fusion.9, f32[24,128,256]{2,1,0:T(8,128)} %fusion.20), kind=kLoop, calls=%fused_computation.25 | loop fusion | flops 4718592 | bytes 12582912 | tf_op jit(solution)/shard_map/convert_element_type | solution.py:54
  31.9 4.1 %collective-permute-start = (bf16[24,128,512]{2,1,0:T(8,128)(2,1)}, bf16[24,128,512]{2,1,0:T(8,128)(2,1)S(1)}, u32[]{:S(2)}, u32[]{:S(2)}) collective-permute-start(bf16[24,128,512]{2,1,0:T(8,128)(2,1)} %fusion.8), channel_id=1, source_target_pairs={{8,0},{16,8},{24,16},{32,24},{40,32},{48,40},{56,48},{64,56},{72,6... | collective-permute-start | bytes 9437192 | tf_op jit(solution)/shard_map/ppermute | solution.py:18
  36.0 2.5 collective-permute-start.1
  38.5 1.9 collective-permute-start.2
  40.4 2.1 collective-permute-start.3
  42.6 60.2 %collective-permute-done = bf16[24,128,512]{2,1,0:T(8,128)(2,1)S(1)} collective-permute-done((bf16[24,128,512]{2,1,0:T(8,128)(2,1)}, bf16[24,128,512]{2,1,0:T(8,128)(2,1)S(1)}, u32[]{:S(2)}, u32[]{:S(2)}) %collective-permute-start) | collective-permute-done | bytes 3145760 | tf_op jit(solution)/shard_map/ppermute | solution.py:18
  102.8 0.4 fusion.50
  103.2 68.7 %collective-permute-done.1 = bf16[24,128,512]{2,1,0:T(8,128)(2,1)} collective-permute-done((bf16[24,128,512]{2,1,0:T(8,128)(2,1)}, bf16[24,128,512]{2,1,0:T(8,128)(2,1)}, u32[]{:S(2)}, u32[]{:S(2)}) %collective-permute-start.1) | collective-permute-done | bytes 3145760 | tf_op jit(solution)/shard_map/ppermute | solution.py:18
  171.9 2.1 fusion.51
  174.0 63.6 %collective-permute-done.2 = bf16[24,128,512]{2,1,0:T(8,128)(2,1)} collective-permute-done((bf16[24,128,512]{2,1,0:T(8,128)(2,1)}, bf16[24,128,512]{2,1,0:T(8,128)(2,1)}, u32[]{:S(2)}, u32[]{:S(2)}) %collective-permute-start.2) | collective-permute-done | bytes 3145760 | tf_op jit(solution)/shard_map/ppermute | solution.py:18
  237.6 2.1 fusion.52
  239.7 36.0 %collective-permute-done.3 = bf16[24,128,512]{2,1,0:T(8,128)(2,1)} collective-permute-done((bf16[24,128,512]{2,1,0:T(8,128)(2,1)}, bf16[24,128,512]{2,1,0:T(8,128)(2,1)}, u32[]{:S(2)}, u32[]{:S(2)}) %collective-permute-start.3) | collective-permute-done | bytes 3145760 | tf_op jit(solution)/shard_map/ppermute | solution.py:18
  275.7 2.1 fusion.53
  277.8 8.5 %fusion = (f32[128,512]{1,0:T(8,128)S(1)}, f32[128,512]{1,0:T(8,128)S(1)}, f32[128,512]{1,0:T(8,128)S(1)}, f32[128,512]{1,0:T(8,128)S(1)}, f32[128,512]{1,0:T(8,...) fusion(bf16[24,128,512]{2,1,0:T(8,128)(2,1)S(1)} %collective-permute-done, ...), kind=kLoop, calls=%fused_computation.16 | loop fusion | flops 63963136 | bytes 30408704 | tf_op jit(solution)/shard_map/wcf,wcf->cf/dot_general | solution.py:59
  286.5 1.3 multiply_add_fusion
  287.9 0.5 fusion.40
  288.4 82.1 %all-reduce.3.cloned.1.call-done = f32[4,128,512]{2,1,0:T(8,128)} async-done(((f32[4,128,512]{2,1,0:T(8,128)}), f32[4,128,512]{2,1,0:T(8,128)}) %all-reduce.3.cloned.1.call-update) | async-done | bytes 1048592 | tf_op jit(solution)/shard_map/psum | solution.py:87
  370.5 2.3 convolution_bitcast_fusion
  372.8 0.7 copy.4
  (16 shorter events, 0.3 us)
Async XLA Ops:
  6.5 363.9 %all-reduce.3.cloned.1.call-start = ((), (), s32[]{:S(2)}) async-start(), calls=%async_computation | async-start | bytes 2097152 | tf_op jit(solution)/shard_map/psum | solution.py:87
  26.9 15.7 %copy-start = (s32[1,4]{1,0:T(1,128)S(1)}, s32[1,4]{1,0:T(1,128)}, u32[]{:S(2)}) copy-start(s32[1,4]{1,0:T(1,128)} %param.5) | copy-start | bytes 52
  31.9 70.9 %collective-permute-start = (bf16[24,128,512]{2,1,0:T(8,128)(2,1)}, bf16[24,128,512]{2,1,0:T(8,128)(2,1)S(1)}, u32[]{:S(2)}, u32[]{:S(2)}) collective-permute-start(bf16[24,128,512]{2,1,0:T(8,128)(2,1)} %fusion.8), channel_id=1, source_target_pairs={{8,0},{16,8},{24,16},{32,24},{40,32},{48,40},{56,48},{64,56},{72,6... | collective-permute-start | bytes 9437192 | tf_op jit(solution)/shard_map/ppermute | solution.py:18
  36.0 135.9 %collective-permute-start.1 = (bf16[24,128,512]{2,1,0:T(8,128)(2,1)}, bf16[24,128,512]{2,1,0:T(8,128)(2,1)}, u32[]{:S(2)}, u32[]{:S(2)}) collective-permute-start(bf16[24,128,512]{2,1,0:T(8,128)(2,1)} %fusion.8), channel_id=1, source_target_pairs={{16,0},{24,8},{32,16},{40,24},{48,32},{56,40},{64,48},{72,56},{80,... | collective-permute-start | bytes 9437192 | tf_op jit(solution)/shard_map/ppermute | solution.py:18
  38.5 199.1 %collective-permute-start.2 = (bf16[24,128,512]{2,1,0:T(8,128)(2,1)}, bf16[24,128,512]{2,1,0:T(8,128)(2,1)}, u32[]{:S(2)}, u32[]{:S(2)}) collective-permute-start(bf16[24,128,512]{2,1,0:T(8,128)(2,1)} %fusion.8), channel_id=1, source_target_pairs={{24,0},{32,8},{40,16},{48,24},{56,32},{64,40},{72,48},{80,56},{88,... | collective-permute-start | bytes 9437192 | tf_op jit(solution)/shard_map/ppermute | solution.py:18
  40.4 235.3 %collective-permute-start.3 = (bf16[24,128,512]{2,1,0:T(8,128)(2,1)}, bf16[24,128,512]{2,1,0:T(8,128)(2,1)}, u32[]{:S(2)}, u32[]{:S(2)}) collective-permute-start(bf16[24,128,512]{2,1,0:T(8,128)(2,1)} %fusion.8), channel_id=1, source_target_pairs={{32,0},{40,8},{48,16},{56,24},{64,32},{72,40},{80,48},{88,56},{96,... | collective-permute-start | bytes 9437192 | tf_op jit(solution)/shard_map/ppermute | solution.py:18
Sparse Core Ops, SparseCore 0:
  288.0 82.4 all-reduce.2
where the time goes:
time: 381 us; the launch traced here: 380 us
  waiting for transfers between devices  311 us (82%)
  other arithmetic  30.3 us (8%)
  between operations  13.6 us (4%)
  starting transfers between devices  10.6 us (3%)
  matrix products  7.9 us (2%)
  local copies, waits for them, and re-layouts  7.39 us (2%)
    ppermute x4, waiting for transfers between devices, shifted(): return lax.ppermute(block, axis, route)  229 us
    psum x1, waiting for transfers between devices, body(): summed = lax.psum(stacks, 'tm')  82.1 us
    ppermute x4, starting transfers between devices, shifted(): return lax.ppermute(block, axis, route)  10.6 us
    dot_general x1, other arithmetic, cross_spectrum(): jnp.einsum('wcf,wcf->cf', own_spec, other_spec, preferred_element_type=jn...  8.46 us
    add x1, other arithmetic, whiten(): smooth + water_level * jnp.mean(amplitude, axis=-1, keepdims=True) + eps  8.23 us
  transfers between devices with their start and end apart: 5, of which 5 were waited for; matrix products, arithmetic and copies ran while one was open for 1% of the time, Pallas kernels for 0%

commit v1 on v0

--- a/solution.py
+++ b/solution.py
@@ -84,7 +84,7 @@
         chosen = (owners == reader + distance).astype(jnp.float32)
         cross = cross_spectrum(own_spec, arrived, bins_count)
         stacks = stacks + chosen[:, None, None] * cross[None, :, :]
-    summed = lax.psum(stacks, "tm")
+    summed = jnp.sum(lax.all_gather(stacks, "tm"), axis=0)
     result = jnp.einsum("pck,kl->plc", summed, inverse, precision=lax.Precision.HIGHEST)
     return result[None]
 

time: 381 us -> 397 us (1.042)
  waiting for transfers between devices: 311 us -> 323 us
  other arithmetic: 30.3 us -> 34.9 us
    all_gather x0 -> x1, waiting for transfers between devices: none -> 94.1 us  [body(): summed = jnp.sum(lax.all_gather(stacks, 'tm'), axis=0)]
    psum x1 -> x0, waiting for transfers between devices: 82.1 us -> none  [body(): summed = lax.psum(stacks, 'tm')]
    reduce_sum x0 -> x1, other arithmetic: none -> 4.54 us  [body(): summed = jnp.sum(lax.all_gather(stacks, 'tm'), axis=0)]
where the time goes in v1:
time: 397 us; the launch traced here: 396 us
  waiting for transfers between devices  323 us (81%)
  other arithmetic  34.9 us (9%)
  between operations  13.6 us (3%)
  starting transfers between devices  10.6 us (3%)
  local copies, waits for them, and re-layouts  7.39 us (2%)
  matrix products  6.69 us (2%)
    ppermute x4, waiting for transfers between devices, shifted(): return lax.ppermute(block, axis, route)  229 us
    all_gather x1, waiting for transfers between devices, body(): summed = jnp.sum(lax.all_gather(stacks, 'tm'), axis=0)  94.1 us
    ppermute x4, starting transfers between devices, shifted(): return lax.ppermute(block, axis, route)  10.6 us
    dot_general x1, other arithmetic, cross_spectrum(): jnp.einsum('wcf,wcf->cf', own_spec, other_spec, preferred_element_type=jn...  8.46 us
    add x1, other arithmetic, whiten(): smooth + water_level * jnp.mean(amplitude, axis=-1, keepdims=True) + eps  8.23 us
  transfers between devices with their start and end apart: 5, of which 5 were waited for; matrix products, arithmetic and copies ran while one was open for 1% of the time, Pallas kernels for 0%

profile of v1, /device:TPU:32, one launch (start us, length us, event | category | flops | bytes accessed | tf_op | source)
XLA Modules:
  0.0 395.8 jit_solution(6343607319746294733)
XLA Ops:
  6.5 4.4 %cosine_convert_fusion = (bf16[1024,256]{1,0:T(8,128)(2,1)S(1)}, bf16[1024,256]{1,0:T(8,128)(2,1)S(1)}) fusion(s32[256]{0:T(256)S(1)} %iota_add_fusion), kind=kLoop, calls=%fused_computation.60 | loop fusion | flops 4456448 | bytes 1049600 | tf_op jit(solution)/shard_map/convert.4
  11.0 0.9 convert_bitcast_fusion
  11.9 5.6 %fusion.9 = f32[24,128,512]{2,1,0:T(8,128)S(1)} fusion(bf16[1,24,128,1024]{3,2,1,0:T(8,128)(2,1)} %param.3, bf16[24,1024]{1,0:T(8,128)(2,1)S(1)} %convert_bitcast_fusion, bf16[1024,256]{1,0:T(8,128)(2,1)S(1)} %get-tuple-element.26, bf16[1024,256]{1,0:T(8,128)(2,1)S(1)} %get-tuple-element.25), kind=kOutput, calls=%fused_computation.27 | convolution fusion | flops 3226468352 | bytes 13680640 | tf_op jit(solution)/shard_map/dot_general | solution.py:41
  17.4 1.2 fusion.48
  18.6 8.2 %fusion.20 = f32[24,128,256]{2,1,0:T(8,128)} fusion(f32[24,128,256]{2,1,0:T(8,128)S(1)} %get-tuple-element.14, f32[24,128]{1,0:T(8,128)S(1)} %broadcast_multiply_fusion), kind=kLoop, calls=%fused_computation.38 | loop fusion | flops 8650752 | bytes 6303744 | tf_op jit(solution)/shard_map/add | solution.py:53
  26.9 5.0 %fusion.8 = bf16[24,128,512]{2,1,0:T(8,128)(2,1)} fusion(f32[24,128,512]{2,1,0:T(8,128)S(1)} %fusion.9, f32[24,128,256]{2,1,0:T(8,128)} %fusion.20), kind=kLoop, calls=%fused_computation.25 | loop fusion | flops 4718592 | bytes 12582912 | tf_op jit(solution)/shard_map/convert_element_type | solution.py:54
  31.9 4.1 %collective-permute-start = (bf16[24,128,512]{2,1,0:T(8,128)(2,1)}, bf16[24,128,512]{2,1,0:T(8,128)(2,1)S(1)}, u32[]{:S(2)}, u32[]{:S(2)}) collective-permute-start(bf16[24,128,512]{2,1,0:T(8,128)(2,1)} %fusion.8), channel_id=1, source_target_pairs={{8,0},{16,8},{24,16},{32,24},{40,32},{48,40},{56,48},{64,56},{72,6... | collective-permute-start | bytes 9437192 | tf_op jit(solution)/shard_map/ppermute | solution.py:18
  36.0 2.5 collective-permute-start.1
  38.5 1.9 collective-permute-start.2
  40.4 2.1 collective-permute-start.3
  42.6 60.2 %collective-permute-done = bf16[24,128,512]{2,1,0:T(8,128)(2,1)S(1)} collective-permute-done((bf16[24,128,512]{2,1,0:T(8,128)(2,1)}, bf16[24,128,512]{2,1,0:T(8,128)(2,1)S(1)}, u32[]{:S(2)}, u32[]{:S(2)}) %collective-permute-start) | collective-permute-done | bytes 3145760 | tf_op jit(solution)/shard_map/ppermute | solution.py:18
  103.2 68.7 %collective-permute-done.1 = bf16[24,128,512]{2,1,0:T(8,128)(2,1)} collective-permute-done((bf16[24,128,512]{2,1,0:T(8,128)(2,1)}, bf16[24,128,512]{2,1,0:T(8,128)(2,1)}, u32[]{:S(2)}, u32[]{:S(2)}) %collective-permute-start.1) | collective-permute-done | bytes 3145760 | tf_op jit(solution)/shard_map/ppermute | solution.py:18
  171.9 2.1 fusion.51
  174.0 63.6 %collective-permute-done.2 = bf16[24,128,512]{2,1,0:T(8,128)(2,1)} collective-permute-done((bf16[24,128,512]{2,1,0:T(8,128)(2,1)}, bf16[24,128,512]{2,1,0:T(8,128)(2,1)}, u32[]{:S(2)}, u32[]{:S(2)}) %collective-permute-start.2) | collective-permute-done | bytes 3145760 | tf_op jit(solution)/shard_map/ppermute | solution.py:18
  237.6 2.1 fusion.52
  239.7 36.0 %collective-permute-done.3 = bf16[24,128,512]{2,1,0:T(8,128)(2,1)} collective-permute-done((bf16[24,128,512]{2,1,0:T(8,128)(2,1)}, bf16[24,128,512]{2,1,0:T(8,128)(2,1)}, u32[]{:S(2)}, u32[]{:S(2)}) %collective-permute-start.3) | collective-permute-done | bytes 3145760 | tf_op jit(solution)/shard_map/ppermute | solution.py:18
  275.7 2.1 fusion.53
  277.8 8.5 %fusion = (f32[128,512]{1,0:T(8,128)S(1)}, f32[128,512]{1,0:T(8,128)S(1)}, f32[128,512]{1,0:T(8,128)S(1)}, f32[128,512]{1,0:T(8,128)S(1)}, f32[128,512]{1,0:T(8,...) fusion(bf16[24,128,512]{2,1,0:T(8,128)(2,1)S(1)} %collective-permute-done, ...), kind=kLoop, calls=%fused_computation.16 | loop fusion | flops 63963136 | bytes 30408704 | tf_op jit(solution)/shard_map/wcf,wcf->cf/dot_general | solution.py:59
  286.5 1.4 multiply_add_fusion
  287.9 0.5 fusion.40
  288.4 94.1 %all-gather.2.cloned.1.call-done = f32[8,4,128,512]{3,2,1,0:T(8,128)} async-done(((f32[1,4,128,512]{3,2,1,0:T(8,128)}), f32[8,4,128,512]{3,2,1,0:T(8,128)}) %all-gather.2.cloned.1.call-update) | async-done | bytes 8388624 | tf_op jit(solution)/shard_map/all_gather | solution.py:87
  382.5 4.5 %reduce_sum.19 = f32[4,128,512]{2,1,0:T(8,128)S(1)} reduce(f32[8,4,128,512]{3,2,1,0:T(8,128)} %all-gather.2.cloned.1.call-done, f32[]{:T(128)} %constant.53.clone.1), dimensions={0}, to_apply=%region_1.2 | reduce | flops 1835008 | bytes 9437188 | tf_op jit(solution)/shard_map/reduce_sum | solution.py:87
  387.1 1.1 convolution_bitcast_fusion
  388.2 0.7 copy.5
  (17 shorter events, 0.6 us)
Async XLA Ops:
  6.5 376.0 %all-gather.2.cloned.1.call-start = ((), (), s32[]{:S(2)}) async-start(), calls=%async_computation | async-start | bytes 9437184 | tf_op jit(solution)/shard_map/all_gather | solution.py:87
  26.9 15.7 %copy-start = (s32[1,4]{1,0:T(1,128)S(1)}, s32[1,4]{1,0:T(1,128)}, u32[]{:S(2)}) copy-start(s32[1,4]{1,0:T(1,128)} %param.5) | copy-start | bytes 52
  31.9 70.9 %collective-permute-start = (bf16[24,128,512]{2,1,0:T(8,128)(2,1)}, bf16[24,128,512]{2,1,0:T(8,128)(2,1)S(1)}, u32[]{:S(2)}, u32[]{:S(2)}) collective-permute-start(bf16[24,128,512]{2,1,0:T(8,128)(2,1)} %fusion.8), channel_id=1, source_target_pairs={{8,0},{16,8},{24,16},{32,24},{40,32},{48,40},{56,48},{64,56},{72,6... | collective-permute-start | bytes 9437192 | tf_op jit(solution)/shard_map/ppermute | solution.py:18
  36.0 135.9 %collective-permute-start.1 = (bf16[24,128,512]{2,1,0:T(8,128)(2,1)}, bf16[24,128,512]{2,1,0:T(8,128)(2,1)}, u32[]{:S(2)}, u32[]{:S(2)}) collective-permute-start(bf16[24,128,512]{2,1,0:T(8,128)(2,1)} %fusion.8), channel_id=1, source_target_pairs={{16,0},{24,8},{32,16},{40,24},{48,32},{56,40},{64,48},{72,56},{80,... | collective-permute-start | bytes 9437192 | tf_op jit(solution)/shard_map/ppermute | solution.py:18
  38.5 199.1 %collective-permute-start.2 = (bf16[24,128,512]{2,1,0:T(8,128)(2,1)}, bf16[24,128,512]{2,1,0:T(8,128)(2,1)}, u32[]{:S(2)}, u32[]{:S(2)}) collective-permute-start(bf16[24,128,512]{2,1,0:T(8,128)(2,1)} %fusion.8), channel_id=1, source_target_pairs={{24,0},{32,8},{40,16},{48,24},{56,32},{64,40},{72,48},{80,56},{88,... | collective-permute-start | bytes 9437192 | tf_op jit(solution)/shard_map/ppermute | solution.py:18
  40.4 235.3 %collective-permute-start.3 = (bf16[24,128,512]{2,1,0:T(8,128)(2,1)}, bf16[24,128,512]{2,1,0:T(8,128)(2,1)}, u32[]{:S(2)}, u32[]{:S(2)}) collective-permute-start(bf16[24,128,512]{2,1,0:T(8,128)(2,1)} %fusion.8), channel_id=1, source_target_pairs={{32,0},{40,8},{48,16},{56,24},{64,32},{72,40},{80,48},{88,56},{96,... | collective-permute-start | bytes 9437192 | tf_op jit(solution)/shard_map/ppermute | solution.py:18
Sparse Core Ops, SparseCore 0:
  288.0 94.4 all-gather.1
